TPU v7x, 32 devices: a whole 2x2x4 slice. The times are simulated.
32 devices in a mesh: ob: 8 (over z, core), pt: 4 (over y, x).
Axes of the slice: x: 2, y: 2, z: 4, core: 2. Of those that a mesh axis runs over, the one named last changes fastest.
Arguments:
- orbitals: float32 [128, 262144], P(('ob', 'pt')), may hold values from -32 to 32, as said below
- potential: float32 [262144], replicated, may hold values from 0 to 2
- cutoff: float32 [1], replicated, may hold values from 0.4 to 1
- eigvec: float32 [128, 128], replicated, may hold values from -3 to 3, as said below
Outputs:
- gram: float32 [128, 128], P(('ob', 'pt'))
- hamil_sub: float32 [128, 128], P(('ob', 'pt'))
- rotated: float32 [128, 262144], P(None, ('ob', 'pt'))
- residual: float32 [128, 262144], P(None, ('ob', 'pt'))
- ritz: float32 [128], replicated
Inputs may be any that keep to these rules, and one draw needn't show every extreme that they name: `orbitals`: each orbital is a rough field whose scale differs from orbital to orbital and from region to region of the grid. `eigvec`: A full-rank matrix with a unit-sized diagonal and independent off-diagonal entries.
All inputs are finite; a program needn't handle non-finite values.
Results may differ from a plain program's by a relative error of at most 0.00027.
Values sent between devices are 32-bit elements; how exact they have to be, the bound alone decides.
A program may use at most 128 MiB of HBM per device.

v0:
```python
import jax
import jax.numpy as jnp
from jax import lax
from jax.sharding import PartitionSpec as P

G = 64
DEGREE = 12
NPTS = 262144
upper_bound = 8.0
quot_eps = 1e-06


def apply_ham(fields, potential):
    points = fields.shape[-1]
    plane_len = G * G
    x_pair = jnp.roll(fields, plane_len, axis=-1) + jnp.roll(fields, -plane_len, axis=-1)
    cube_view = fields.reshape(fields.shape[0], G, plane_len)
    y_pair = (jnp.roll(cube_view, G, axis=-1) + jnp.roll(cube_view, -G, axis=-1)).reshape(
        fields.shape
    )
    z_index = lax.broadcasted_iota(jnp.int32, (1, points), 1) % G
    z_lower = jnp.where(
        z_index == 0, jnp.roll(fields, 1 - G, axis=-1), jnp.roll(fields, 1, axis=-1)
    )
    z_upper = jnp.where(
        z_index == G - 1, jnp.roll(fields, G - 1, axis=-1), jnp.roll(fields, -1, axis=-1)
    )
    return -0.5 * (x_pair + y_pair + z_lower + z_upper - 6.0 * fields) + potential * fields


def chebyshev(fields, potential, cutoff):
    center = 0.5 * (upper_bound + cutoff[0])
    half_width = 0.5 * (upper_bound - cutoff[0])
    current = (apply_ham(fields, potential) - center * fields) / half_width

    def advance(turn_idx, carry):
        previous, present = carry
        following = 2.0 * (apply_ham(present, potential) - center * present) / half_width - previous
        return (present, following)

    previous, current = lax.fori_loop(0, DEGREE - 1, advance, (fields, current))
    return (current, apply_ham(current, potential))


def on_device(orbitals, potential, cutoff, eigvec):
    high = lax.Precision.HIGHEST
    filtered, applied = chebyshev(orbitals, potential, cutoff)
    total_orb = eigvec.shape[0]
    n_ob = lax.axis_size("ob")
    n_pt = lax.axis_size("pt")
    per_dev = total_orb // (n_ob * n_pt)
    rows_filt, rows_appl = (
        lax.all_to_all(filtered, ("ob", "pt"), split_axis=1, concat_axis=0, tiled=True),
        lax.all_to_all(applied, ("ob", "pt"), split_axis=1, concat_axis=0, tiled=True),
    )
    part_gram = jnp.dot(rows_filt, rows_filt.T, precision=high) / NPTS
    part_hamil = jnp.dot(rows_filt, rows_appl.T, precision=high) / NPTS
    gram, hamil_sub = (
        lax.psum_scatter(part_gram, ("ob", "pt"), scatter_dimension=0, tiled=True),
        lax.psum_scatter(part_hamil, ("ob", "pt"), scatter_dimension=0, tiled=True),
    )
    rotated = jnp.dot(eigvec.T, rows_filt, precision=high)
    rot_applied = jnp.dot(eigvec.T, rows_appl, precision=high)
    my_index = lax.axis_index(("ob", "pt"))
    my_rows = lax.dynamic_slice_in_dim(eigvec, my_index * per_dev, per_dev, 0)
    numer = jnp.sum(my_rows * jnp.dot(hamil_sub, eigvec, precision=high), axis=0)
    denom = jnp.sum(my_rows * jnp.dot(gram, eigvec, precision=high), axis=0)
    numer, denom = lax.psum((numer, denom), ("ob", "pt"))
    ritz = numer / (denom + quot_eps)
    residual = rot_applied - ritz[:, None] * rotated
    return (gram, hamil_sub, rotated, residual, ritz)


def solution(mesh):
    return jax.shard_map(
        on_device,
        mesh=mesh,
        in_specs=(P(("ob", "pt"), None), P(), P(), P()),
        out_specs=(
            P(("ob", "pt"), None),
            P(("ob", "pt"), None),
            P(None, ("ob", "pt")),
            P(None, ("ob", "pt")),
            P(),
        ),
        check_vma=False,
    )
```

profile of v0, /device:TPU:0, one launch (start us, length us, event | category | flops | bytes accessed | tf_op | source)
XLA Modules:
  0.0 1040.0 jit_solution(13240792252912524412)
XLA Ops:
  13.5 4.6 fusion.57
  28.6 4.7 copy.22
  33.3 24.7 %fusion.29 = f32[4,262144]{1,0:T(4,128)} fusion(f32[4,262144]{1,0:T(4,128)} %copy-done.2, f32[4,1]{1,0:T(4,128)S(1)} %get-tuple-element.162, f32[4,262143]{1,0:T(4,128)} %get-tuple-element.164, f32[4,262081]{1,0:T(4,128)} %get-tuple-element.158, f32[4,63]{1,0:T(4,128)S(1)} %get-tuple-element.160, f32[4,262143]{1,0:T(4,128)} %get-tuple-element.163, ...), kind=kLoop, calls=%fused_computation.49 | loop fusion | flops 20971520 | bytes 39321608 | tf_op jit(solution)/shard_map/div | solution.py:34
  58.0 528.4 %while.14 = (s32[]{:T(128)}, f32[4,262144]{1,0:T(4,128)}, f32[4,262144]{1,0:T(4,128)}, f32[262144]{0:T(1024)S(1)}, f32[]{:T(128)}, /*index=5*/f32[]{:T(128)}, s32[]{:T(128)}) while((s32[]{:T(128)}, f32[4,262144]{1,0:T(4,128)}, f32[4,262144]{1,0:T(4,128)}, f32[262144]{0:T(1024)S(1)}, f32[]{:T(128)}, /*index=5*/f32[]{:T(128)}, s32[]{:T(128)}) %tuple.84), condition=%wide.region_1.2_spmd, body=%wide.region_0.1_spmd.sunk | while | flops 28311552 | bytes 190840976 | solution.py:41
  58.3 4.6 copy.33
  81.5 20.9 %divide_subtract_fusion.2 = f32[4,262144]{1,0:T(4,128)S(1)} fusion(f32[4,262144]{1,0:T(4,128)S(1)} %copy-done.3, f32[4,262144]{1,0:T(4,128)S(1)} %copy-done, f32[4,1]{1,0:T(4,128)S(1)} %get-tuple-element.222, f32[4,262143]{1,0:T(4,128)} %get-tuple-element.223, f32[4,262081]{1,0:T(4,128)} %get-tuple-element.224, f32[4,63]{1,0:T(4,128)S(1)} %get-tuple-element.225, ...), kind=kLoop, calls=%fused_computation.clone.1 | loop fusion | flops 23068672 | bytes 43515912 | tf_op jit(solution)/shard_map/while/body/eval_jaxpr/sub | solution.py:38
  129.5 20.9 %divide_subtract_fusion.2 = f32[4,262144]{1,0:T(4,128)S(1)} fusion(f32[4,262144]{1,0:T(4,128)S(1)} %copy-done.3, f32[4,262144]{1,0:T(4,128)S(1)} %copy-done, f32[4,1]{1,0:T(4,128)S(1)} %get-tuple-element.222, f32[4,262143]{1,0:T(4,128)} %get-tuple-element.223, f32[4,262081]{1,0:T(4,128)} %get-tuple-element.224, f32[4,63]{1,0:T(4,128)S(1)} %get-tuple-element.225, ...), kind=kLoop, calls=%fused_computation.clone.1 | loop fusion | flops 23068672 | bytes 43515912 | tf_op jit(solution)/shard_map/while/body/eval_jaxpr/sub | solution.py:38
  177.5 20.9 %divide_subtract_fusion.2 = f32[4,262144]{1,0:T(4,128)S(1)} fusion(f32[4,262144]{1,0:T(4,128)S(1)} %copy-done.3, f32[4,262144]{1,0:T(4,128)S(1)} %copy-done, f32[4,1]{1,0:T(4,128)S(1)} %get-tuple-element.222, f32[4,262143]{1,0:T(4,128)} %get-tuple-element.223, f32[4,262081]{1,0:T(4,128)} %get-tuple-element.224, f32[4,63]{1,0:T(4,128)S(1)} %get-tuple-element.225, ...), kind=kLoop, calls=%fused_computation.clone.1 | loop fusion | flops 23068672 | bytes 43515912 | tf_op jit(solution)/shard_map/while/body/eval_jaxpr/sub | solution.py:38
  225.5 20.9 %divide_subtract_fusion.2 = f32[4,262144]{1,0:T(4,128)S(1)} fusion(f32[4,262144]{1,0:T(4,128)S(1)} %copy-done.3, f32[4,262144]{1,0:T(4,128)S(1)} %copy-done, f32[4,1]{1,0:T(4,128)S(1)} %get-tuple-element.222, f32[4,262143]{1,0:T(4,128)} %get-tuple-element.223, f32[4,262081]{1,0:T(4,128)} %get-tuple-element.224, f32[4,63]{1,0:T(4,128)S(1)} %get-tuple-element.225, ...), kind=kLoop, calls=%fused_computation.clone.1 | loop fusion | flops 23068672 | bytes 43515912 | tf_op jit(solution)/shard_map/while/body/eval_jaxpr/sub | solution.py:38
  250.3 4.6 copy.33
  273.5 20.9 %divide_subtract_fusion.2 = f32[4,262144]{1,0:T(4,128)S(1)} fusion(f32[4,262144]{1,0:T(4,128)S(1)} %copy-done.3, f32[4,262144]{1,0:T(4,128)S(1)} %copy-done, f32[4,1]{1,0:T(4,128)S(1)} %get-tuple-element.222, f32[4,262143]{1,0:T(4,128)} %get-tuple-element.223, f32[4,262081]{1,0:T(4,128)} %get-tuple-element.224, f32[4,63]{1,0:T(4,128)S(1)} %get-tuple-element.225, ...), kind=kLoop, calls=%fused_computation.clone.1 | loop fusion | flops 23068672 | bytes 43515912 | tf_op jit(solution)/shard_map/while/body/eval_jaxpr/sub | solution.py:38
  298.3 4.6 copy.33
  321.4 20.9 %divide_subtract_fusion.2 = f32[4,262144]{1,0:T(4,128)S(1)} fusion(f32[4,262144]{1,0:T(4,128)S(1)} %copy-done.3, f32[4,262144]{1,0:T(4,128)S(1)} %copy-done, f32[4,1]{1,0:T(4,128)S(1)} %get-tuple-element.222, f32[4,262143]{1,0:T(4,128)} %get-tuple-element.223, f32[4,262081]{1,0:T(4,128)} %get-tuple-element.224, f32[4,63]{1,0:T(4,128)S(1)} %get-tuple-element.225, ...), kind=kLoop, calls=%fused_computation.clone.1 | loop fusion | flops 23068672 | bytes 43515912 | tf_op jit(solution)/shard_map/while/body/eval_jaxpr/sub | solution.py:38
  346.3 4.6 copy.33
  369.4 20.9 %divide_subtract_fusion.2 = f32[4,262144]{1,0:T(4,128)S(1)} fusion(f32[4,262144]{1,0:T(4,128)S(1)} %copy-done.3, f32[4,262144]{1,0:T(4,128)S(1)} %copy-done, f32[4,1]{1,0:T(4,128)S(1)} %get-tuple-element.222, f32[4,262143]{1,0:T(4,128)} %get-tuple-element.223, f32[4,262081]{1,0:T(4,128)} %get-tuple-element.224, f32[4,63]{1,0:T(4,128)S(1)} %get-tuple-element.225, ...), kind=kLoop, calls=%fused_computation.clone.1 | loop fusion | flops 23068672 | bytes 43515912 | tf_op jit(solution)/shard_map/while/body/eval_jaxpr/sub | solution.py:38
  417.4 20.9 %divide_subtract_fusion.2 = f32[4,262144]{1,0:T(4,128)S(1)} fusion(f32[4,262144]{1,0:T(4,128)S(1)} %copy-done.3, f32[4,262144]{1,0:T(4,128)S(1)} %copy-done, f32[4,1]{1,0:T(4,128)S(1)} %get-tuple-element.222, f32[4,262143]{1,0:T(4,128)} %get-tuple-element.223, f32[4,262081]{1,0:T(4,128)} %get-tuple-element.224, f32[4,63]{1,0:T(4,128)S(1)} %get-tuple-element.225, ...), kind=kLoop, calls=%fused_computation.clone.1 | loop fusion | flops 23068672 | bytes 43515912 | tf_op jit(solution)/shard_map/while/body/eval_jaxpr/sub | solution.py:38
  465.4 20.9 %divide_subtract_fusion.2 = f32[4,262144]{1,0:T(4,128)S(1)} fusion(f32[4,262144]{1,0:T(4,128)S(1)} %copy-done.3, f32[4,262144]{1,0:T(4,128)S(1)} %copy-done, f32[4,1]{1,0:T(4,128)S(1)} %get-tuple-element.222, f32[4,262143]{1,0:T(4,128)} %get-tuple-element.223, f32[4,262081]{1,0:T(4,128)} %get-tuple-element.224, f32[4,63]{1,0:T(4,128)S(1)} %get-tuple-element.225, ...), kind=kLoop, calls=%fused_computation.clone.1 | loop fusion | flops 23068672 | bytes 43515912 | tf_op jit(solution)/shard_map/while/body/eval_jaxpr/sub | solution.py:38
  513.4 20.9 %divide_subtract_fusion.2 = f32[4,262144]{1,0:T(4,128)S(1)} fusion(f32[4,262144]{1,0:T(4,128)S(1)} %copy-done.3, f32[4,262144]{1,0:T(4,128)S(1)} %copy-done, f32[4,1]{1,0:T(4,128)S(1)} %get-tuple-element.222, f32[4,262143]{1,0:T(4,128)} %get-tuple-element.223, f32[4,262081]{1,0:T(4,128)} %get-tuple-element.224, f32[4,63]{1,0:T(4,128)S(1)} %get-tuple-element.225, ...), kind=kLoop, calls=%fused_computation.clone.1 | loop fusion | flops 23068672 | bytes 43515912 | tf_op jit(solution)/shard_map/while/body/eval_jaxpr/sub | solution.py:38
  561.4 20.9 %divide_subtract_fusion.2 = f32[4,262144]{1,0:T(4,128)S(1)} fusion(f32[4,262144]{1,0:T(4,128)S(1)} %copy-done.3, f32[4,262144]{1,0:T(4,128)S(1)} %copy-done, f32[4,1]{1,0:T(4,128)S(1)} %get-tuple-element.222, f32[4,262143]{1,0:T(4,128)} %get-tuple-element.223, f32[4,262081]{1,0:T(4,128)} %get-tuple-element.224, f32[4,63]{1,0:T(4,128)S(1)} %get-tuple-element.225, ...), kind=kLoop, calls=%fused_computation.clone.1 | loop fusion | flops 23068672 | bytes 43515912 | tf_op jit(solution)/shard_map/while/body/eval_jaxpr/sub | solution.py:38
  586.3 4.6 copy.29
  609.9 23.3 %fusion.27 = f32[4,262144]{1,0:T(4,128)S(1)} fusion(f32[4,262144]{1,0:T(4,128)S(1)} %bitcast.66, f32[4,258048]{1,0:T(4,128)} %get-tuple-element.142, f32[4,4096]{1,0:T(4,128)S(1)} %get-tuple-element.144, f32[4,4096]{1,0:T(4,128)S(1)} %get-tuple-element.143, f32[4,258048]{1,0:T(4,128)} %get-tuple-element.141, f32[4,63]{1,0:T(4,128)S(1)} %get-tuple-element.138, ...), kind=kLoop, calls=%fused_computation.44 | loop fusion | flops 17825792 | bytes 39321600 | tf_op jit(solution)/shard_map/add | solution.py:28
  633.2 101.2 %all_to_all.38 = f32[4,32,8192]{2,0,1:T(4,128)} all-to-all(f32[4,32,8192]{2,0,1:T(4,128)S(1)} %bitcast.67), channel_id=1, replica_groups=mesh['ob'=8,'pt'=4] {'ob','pt'}, dimensions={1} | all-to-all | bytes 8388608 | tf_op jit(solution)/shard_map/all_to_all | solution.py:54
  738.0 5.5 all_to_all.35
  743.6 88.6 %all-to-all-done = f32[4,32,8192]{2,0,1:T(4,128)} async-done(((f32[4,32,8192]{2,0,1:T(4,128)}), f32[4,32,8192]{2,0,1:T(4,128)}, u32[]{:S(2)}, u32[]{:S(2)}) %all-to-all-start) | async-done | bytes 4194336 | tf_op jit(solution)/shard_map/all_to_all | solution.py:53
  832.1 5.3 all_to_all.31
  837.4 7.7 convolution_multiply_fusion.1
  849.3 9.9 convolution_bitcast_fusion.1
  859.1 5.6 copy.17
  864.7 110.7 %all-reduce.6.cloned.1.call-done = (f32[128,128]{1,0:T(8,128)}, f32[128,128]{1,0:T(8,128)}) async-done(((f32[128,128]{1,0:T(8,128)}, f32[128,128]{1,0:T(8,128)}), (f32[128,128]{1,0:T(8,128)}, f32[128,128]{1,0:T(8,128)})) %all-reduce.6.cloned.1.call-update) | async-done | bytes 131088
  977.1 39.6 %all-reduce.2 = (f32[128]{0:T(128)S(1)}, f32[128]{0:T(128)S(1)}) all-reduce(f32[128]{0:T(128)S(1)} %fusion.30, f32[128]{0:T(128)S(1)} %fusion.31), channel_id=1, replica_groups=mesh['ob'=8,'pt'=4] {'ob','pt'}, use_global_device_ids=true, to_apply=%region_5.6 | all-reduce | flops 256 | bytes 2048 | tf_op jit(solution)/shard_map/psum | solution.py:68
  1016.7 10.5 %fusion.13 = f32[128,8192]{0,1:T(8,128)} fusion(f32[128,8192]{1,0:T(8,128)} %all_to_all.35, f32[128,128]{1,0:T(8,128)S(1)} %copy-done.12, f32[128,8192]{0,1:T(8,128)} %convolution_bitcast_fusion.1, f32[128]{0:T(128)S(1)} %add_divide_fusion), kind=kOutput, calls=%fused_computation.22 | convolution fusion | flops 1612709888 | bytes 12648960 | tf_op jit(solution)/shard_map/dot_general | solution.py:63
  1027.2 5.6 copy.18
  (252 shorter events, 323.4 us)
Async XLA Ops:
  9.4 16.8 %copy-start.2 = (f32[4,262144]{1,0:T(4,128)}, f32[4,262144]{1,0:T(4,128)S(1)}, u32[]{:S(2)}) copy-start(f32[4,262144]{1,0:T(4,128)S(1)} %copy.48) | copy-start | bytes 12582916
  26.6 6.7 copy-start.8
  26.6 6.7 copy-start.10
  28.6 4.7 copy-start.5
  76.9 4.6 copy-start.3
  113.9 2.7 copy-start
  124.8 4.6 copy-start.3
  161.9 2.7 copy-start
  172.8 4.6 copy-start.3
  209.9 2.7 copy-start
  220.8 4.6 copy-start.3
  257.9 2.7 copy-start
  268.8 4.6 copy-start.3
  316.8 4.6 copy-start.3
  364.8 4.6 copy-start.3
  401.8 2.7 copy-start
  412.8 4.6 copy-start.3
  449.8 2.7 copy-start
  460.7 4.6 copy-start.3
  508.7 4.6 copy-start.3
  556.7 4.6 copy-start.3
  607.1 2.7 copy-start.7
  607.1 2.7 copy-start.9
  607.1 2.7 copy-start.11
  734.4 97.7 %all-to-all-start = ((f32[4,32,8192]{2,0,1:T(4,128)}), f32[4,32,8192]{2,0,1:T(4,128)}, u32[]{:S(2)}, u32[]{:S(2)}) async-start(f32[4,32,8192]{2,0,1:T(4,128)} %bitcast.55), calls=%async_computation | async-start | bytes 8388608 | tf_op jit(solution)/shard_map/all_to_all | solution.py:53
  738.0 237.4 %all-reduce.6.cloned.1.call-start = ((), (), s32[]{:S(2)}) async-start(), calls=%async_computation.2 | async-start | bytes 262144
  837.4 7.7 copy-start.4
  837.4 7.7 copy-start.6
  845.1 4.1 copy-start.12
  976.1 51.1 %copy-start.13 = (f32[4,128]{1,0:T(4,128)}, f32[4,128]{1,0:T(4,128)S(1)}, u32[]{:S(2)}) copy-start(f32[4,128]{1,0:T(4,128)S(1)} %constant_dynamic-slice_fusion) | copy-start | bytes 6148
  976.8 50.5 %copy-start.14 = (f32[4,128]{1,0:T(4,128)}, f32[4,128]{1,0:T(4,128)S(1)}, u32[]{:S(2)}) copy-start(f32[4,128]{1,0:T(4,128)S(1)} %constant_dynamic-slice_fusion.1) | copy-start | bytes 6148
  1016.7 10.5 %copy-start.15 = (f32[128]{0:T(128)}, f32[128]{0:T(128)S(1)}, u32[]{:S(2)}) copy-start(f32[128]{0:T(128)S(1)} %add_divide_fusion) | copy-start | bytes 1540
  (6 other events, 15.8 us)
Sparse Core Ops, SparseCore 0:
  849.4 125.9 all-reduce.5
where the time goes:
time: 1040 us
  local copies, waits for them, and re-layouts  349 us (34%)
  other arithmetic  299 us (29%)
  waiting for transfers between devices  199 us (19%)
  blocking collectives  141 us (14%)
  matrix products  32.6 us (3%)
  between operations  15.2 us (1%)
    sub x11, other arithmetic, advance(): 2.0 * (apply_ham(present, potential) - center * present) / half_width  229 us
    while x88, local copies, waits for them, and re-layouts  124 us
    unnamed x2, waiting for transfers between devices  111 us
    all_to_all x1, blocking collectives, on_device(): lax.all_to_all(applied, ('ob', 'pt'), split_axis=1, concat_axis=0, tiled=...  101 us
    all_to_all x1, waiting for transfers between devices, on_device(): lax.all_to_all(filtered, ('ob', 'pt'), split_axis=1, concat_axis=0, tiled...  88.6 us
    slice x24, local copies, waits for them, and re-layouts, apply_ham(): jnp.roll(fields, 1 - G, axis=-1)  54.5 us
    slice x24, local copies, waits for them, and re-layouts, apply_ham(): jnp.roll(fields, plane_len, axis=-1) + jnp.roll(fields, -plane_len, axis=-1)  49.1 us
    slice x24, local copies, waits for them, and re-layouts, apply_ham(): jnp.roll(fields, 1, axis=-1)  46.4 us
  transfers between devices with their start and end apart: 2, of which 2 were waited for; matrix products, arithmetic and copies ran while one was open for 1% of the time, Pallas kernels for 0%

commit v1 on v0

--- a/solution.py
+++ b/solution.py
@@ -51,7 +51,15 @@
     per_dev = total_orb // (n_ob * n_pt)
     rows_filt, rows_appl = (
         lax.all_to_all(filtered, ("ob", "pt"), split_axis=1, concat_axis=0, tiled=True),
-        lax.all_to_all(applied, ("ob", "pt"), split_axis=1, concat_axis=0, tiled=True),
+        jnp.concatenate(
+            lax.all_to_all(
+                jnp.stack(jnp.split(applied, lax.axis_size(("ob", "pt")), axis=1)),
+                ("ob", "pt"),
+                0,
+                0,
+            ),
+            axis=0,
+        ),
     )
     part_gram = jnp.dot(rows_filt, rows_filt.T, precision=high) / NPTS
     part_hamil = jnp.dot(rows_filt, rows_appl.T, precision=high) / NPTS

time: 1040 us -> 997 us (0.959)
  blocking collectives: 141 us -> 39.5 us
  local copies, waits for them, and re-layouts: 349 us -> 370 us
  waiting for transfers between devices: 199 us -> 218 us
    all_to_all x1 -> x0, blocking collectives: 101 us -> none  [on_device(): lax.all_to_all(applied, ('ob', 'pt'), split_axis=1, concat_axis=0, tiled=...]
    all_to_all x0 -> x1, waiting for transfers between devices: none -> 81 us  [on_device(): lax.all_to_all(jnp.stack(jnp.split(applied, lax.axis_size(('ob', 'pt')),...]
    all_to_all x1, waiting for transfers between devices: 88.6 us -> 26.1 us  [on_device(): lax.all_to_all(filtered, ('ob', 'pt'), split_axis=1, concat_axis=0, tiled...]
    unnamed x37 -> x64, local copies, waits for them, and re-layouts: 29.7 us -> 50.3 us
  transfers between devices with their start and end apart: 2 -> 3, of which waited for: 2 -> 3; matrix products, arithmetic and copies ran while one was open for 1% -> 9% of each run, Pallas kernels for 0% -> 0%
where the time goes in v1:
time: 997 us; the launch traced here: 992 us
  local copies, waits for them, and re-layouts  370 us (37%)
  other arithmetic  299 us (30%)
  waiting for transfers between devices  218 us (22%)
  blocking collectives  39.5 us (4%)
  matrix products  35.9 us (4%)
  between operations  15.2 us (2%)
  starting transfers between devices  13.5 us (1%)
    sub x11, other arithmetic, advance(): 2.0 * (apply_ham(present, potential) - center * present) / half_width  229 us
    while x88, local copies, waits for them, and re-layouts  124 us
    unnamed x2, waiting for transfers between devices  111 us
    all_to_all x1, waiting for transfers between devices, on_device(): lax.all_to_all(jnp.stack(jnp.split(applied, lax.axis_size(('ob', 'pt')),...  81 us
    slice x24, local copies, waits for them, and re-layouts, apply_ham(): jnp.roll(fields, 1 - G, axis=-1)  54.5 us
    unnamed x64, local copies, waits for them, and re-layouts  50.3 us
    slice x24, local copies, waits for them, and re-layouts, apply_ham(): jnp.roll(fields, plane_len, axis=-1) + jnp.roll(fields, -plane_len, axis=-1)  49.1 us
    slice x24, local copies, waits for them, and re-layouts, apply_ham(): jnp.roll(fields, 1, axis=-1)  46.4 us
  transfers between devices with their start and end apart: 3, of which 3 were waited for; matrix products, arithmetic and copies ran while one was open for 9% of the time, Pallas kernels for 0%

profile of v1, /device:TPU:0, one launch (start us, length us, event | category | flops | bytes accessed | tf_op | source)
XLA Modules:
  0.0 991.9 jit_solution(12467556831801859708)
XLA Ops:
  13.5 4.6 fusion.89
  28.6 4.7 copy.20
  33.3 24.7 %fusion.29 = f32[4,262144]{1,0:T(4,128)} fusion(f32[4,262144]{1,0:T(4,128)} %copy-done.2, f32[4,1]{1,0:T(4,128)S(1)} %get-tuple-element.162, f32[4,262143]{1,0:T(4,128)} %get-tuple-element.164, f32[4,262081]{1,0:T(4,128)} %get-tuple-element.158, f32[4,63]{1,0:T(4,128)S(1)} %get-tuple-element.160, f32[4,262143]{1,0:T(4,128)} %get-tuple-element.163, ...), kind=kLoop, calls=%fused_computation.49 | loop fusion | flops 20971520 | bytes 39321608 | tf_op jit(solution)/shard_map/div | solution.py:34
  58.0 528.4 %while.14 = (s32[]{:T(128)}, f32[4,262144]{1,0:T(4,128)}, f32[4,262144]{1,0:T(4,128)}, f32[262144]{0:T(1024)S(1)}, f32[]{:T(128)}, /*index=5*/f32[]{:T(128)}, s32[]{:T(128)}) while((s32[]{:T(128)}, f32[4,262144]{1,0:T(4,128)}, f32[4,262144]{1,0:T(4,128)}, f32[262144]{0:T(1024)S(1)}, f32[]{:T(128)}, /*index=5*/f32[]{:T(128)}, s32[]{:T(128)}) %tuple.84), condition=%wide.region_1.2_spmd, body=%wide.region_0.1_spmd.sunk | while | flops 28311552 | bytes 190840976 | solution.py:41
  58.3 4.6 copy.31
  81.5 20.9 %divide_subtract_fusion.2 = f32[4,262144]{1,0:T(4,128)S(1)} fusion(f32[4,262144]{1,0:T(4,128)S(1)} %copy-done.3, f32[4,262144]{1,0:T(4,128)S(1)} %copy-done, f32[4,1]{1,0:T(4,128)S(1)} %get-tuple-element.222, f32[4,262143]{1,0:T(4,128)} %get-tuple-element.223, f32[4,262081]{1,0:T(4,128)} %get-tuple-element.224, f32[4,63]{1,0:T(4,128)S(1)} %get-tuple-element.225, ...), kind=kLoop, calls=%fused_computation.clone.1 | loop fusion | flops 23068672 | bytes 43515912 | tf_op jit(solution)/shard_map/while/body/eval_jaxpr/sub | solution.py:38
  129.5 20.9 %divide_subtract_fusion.2 = f32[4,262144]{1,0:T(4,128)S(1)} fusion(f32[4,262144]{1,0:T(4,128)S(1)} %copy-done.3, f32[4,262144]{1,0:T(4,128)S(1)} %copy-done, f32[4,1]{1,0:T(4,128)S(1)} %get-tuple-element.222, f32[4,262143]{1,0:T(4,128)} %get-tuple-element.223, f32[4,262081]{1,0:T(4,128)} %get-tuple-element.224, f32[4,63]{1,0:T(4,128)S(1)} %get-tuple-element.225, ...), kind=kLoop, calls=%fused_computation.clone.1 | loop fusion | flops 23068672 | bytes 43515912 | tf_op jit(solution)/shard_map/while/body/eval_jaxpr/sub | solution.py:38
  177.5 20.9 %divide_subtract_fusion.2 = f32[4,262144]{1,0:T(4,128)S(1)} fusion(f32[4,262144]{1,0:T(4,128)S(1)} %copy-done.3, f32[4,262144]{1,0:T(4,128)S(1)} %copy-done, f32[4,1]{1,0:T(4,128)S(1)} %get-tuple-element.222, f32[4,262143]{1,0:T(4,128)} %get-tuple-element.223, f32[4,262081]{1,0:T(4,128)} %get-tuple-element.224, f32[4,63]{1,0:T(4,128)S(1)} %get-tuple-element.225, ...), kind=kLoop, calls=%fused_computation.clone.1 | loop fusion | flops 23068672 | bytes 43515912 | tf_op jit(solution)/shard_map/while/body/eval_jaxpr/sub | solution.py:38
  225.5 20.9 %divide_subtract_fusion.2 = f32[4,262144]{1,0:T(4,128)S(1)} fusion(f32[4,262144]{1,0:T(4,128)S(1)} %copy-done.3, f32[4,262144]{1,0:T(4,128)S(1)} %copy-done, f32[4,1]{1,0:T(4,128)S(1)} %get-tuple-element.222, f32[4,262143]{1,0:T(4,128)} %get-tuple-element.223, f32[4,262081]{1,0:T(4,128)} %get-tuple-element.224, f32[4,63]{1,0:T(4,128)S(1)} %get-tuple-element.225, ...), kind=kLoop, calls=%fused_computation.clone.1 | loop fusion | flops 23068672 | bytes 43515912 | tf_op jit(solution)/shard_map/while/body/eval_jaxpr/sub | solution.py:38
  273.5 20.9 %divide_subtract_fusion.2 = f32[4,262144]{1,0:T(4,128)S(1)} fusion(f32[4,262144]{1,0:T(4,128)S(1)} %copy-done.3, f32[4,262144]{1,0:T(4,128)S(1)} %copy-done, f32[4,1]{1,0:T(4,128)S(1)} %get-tuple-element.222, f32[4,262143]{1,0:T(4,128)} %get-tuple-element.223, f32[4,262081]{1,0:T(4,128)} %get-tuple-element.224, f32[4,63]{1,0:T(4,128)S(1)} %get-tuple-element.225, ...), kind=kLoop, calls=%fused_computation.clone.1 | loop fusion | flops 23068672 | bytes 43515912 | tf_op jit(solution)/shard_map/while/body/eval_jaxpr/sub | solution.py:38
  321.4 20.9 %divide_subtract_fusion.2 = f32[4,262144]{1,0:T(4,128)S(1)} fusion(f32[4,262144]{1,0:T(4,128)S(1)} %copy-done.3, f32[4,262144]{1,0:T(4,128)S(1)} %copy-done, f32[4,1]{1,0:T(4,128)S(1)} %get-tuple-element.222, f32[4,262143]{1,0:T(4,128)} %get-tuple-element.223, f32[4,262081]{1,0:T(4,128)} %get-tuple-element.224, f32[4,63]{1,0:T(4,128)S(1)} %get-tuple-element.225, ...), kind=kLoop, calls=%fused_computation.clone.1 | loop fusion | flops 23068672 | bytes 43515912 | tf_op jit(solution)/shard_map/while/body/eval_jaxpr/sub | solution.py:38
  369.4 20.9 %divide_subtract_fusion.2 = f32[4,262144]{1,0:T(4,128)S(1)} fusion(f32[4,262144]{1,0:T(4,128)S(1)} %copy-done.3, f32[4,262144]{1,0:T(4,128)S(1)} %copy-done, f32[4,1]{1,0:T(4,128)S(1)} %get-tuple-element.222, f32[4,262143]{1,0:T(4,128)} %get-tuple-element.223, f32[4,262081]{1,0:T(4,128)} %get-tuple-element.224, f32[4,63]{1,0:T(4,128)S(1)} %get-tuple-element.225, ...), kind=kLoop, calls=%fused_computation.clone.1 | loop fusion | flops 23068672 | bytes 43515912 | tf_op jit(solution)/shard_map/while/body/eval_jaxpr/sub | solution.py:38
  417.4 20.9 %divide_subtract_fusion.2 = f32[4,262144]{1,0:T(4,128)S(1)} fusion(f32[4,262144]{1,0:T(4,128)S(1)} %copy-done.3, f32[4,262144]{1,0:T(4,128)S(1)} %copy-done, f32[4,1]{1,0:T(4,128)S(1)} %get-tuple-element.222, f32[4,262143]{1,0:T(4,128)} %get-tuple-element.223, f32[4,262081]{1,0:T(4,128)} %get-tuple-element.224, f32[4,63]{1,0:T(4,128)S(1)} %get-tuple-element.225, ...), kind=kLoop, calls=%fused_computation.clone.1 | loop fusion | flops 23068672 | bytes 43515912 | tf_op jit(solution)/shard_map/while/body/eval_jaxpr/sub | solution.py:38
  465.4 20.9 %divide_subtract_fusion.2 = f32[4,262144]{1,0:T(4,128)S(1)} fusion(f32[4,262144]{1,0:T(4,128)S(1)} %copy-done.3, f32[4,262144]{1,0:T(4,128)S(1)} %copy-done, f32[4,1]{1,0:T(4,128)S(1)} %get-tuple-element.222, f32[4,262143]{1,0:T(4,128)} %get-tuple-element.223, f32[4,262081]{1,0:T(4,128)} %get-tuple-element.224, f32[4,63]{1,0:T(4,128)S(1)} %get-tuple-element.225, ...), kind=kLoop, calls=%fused_computation.clone.1 | loop fusion | flops 23068672 | bytes 43515912 | tf_op jit(solution)/shard_map/while/body/eval_jaxpr/sub | solution.py:38
  513.4 20.9 %divide_subtract_fusion.2 = f32[4,262144]{1,0:T(4,128)S(1)} fusion(f32[4,262144]{1,0:T(4,128)S(1)} %copy-done.3, f32[4,262144]{1,0:T(4,128)S(1)} %copy-done, f32[4,1]{1,0:T(4,128)S(1)} %get-tuple-element.222, f32[4,262143]{1,0:T(4,128)} %get-tuple-element.223, f32[4,262081]{1,0:T(4,128)} %get-tuple-element.224, f32[4,63]{1,0:T(4,128)S(1)} %get-tuple-element.225, ...), kind=kLoop, calls=%fused_computation.clone.1 | loop fusion | flops 23068672 | bytes 43515912 | tf_op jit(solution)/shard_map/while/body/eval_jaxpr/sub | solution.py:38
  561.4 20.9 %divide_subtract_fusion.2 = f32[4,262144]{1,0:T(4,128)S(1)} fusion(f32[4,262144]{1,0:T(4,128)S(1)} %copy-done.3, f32[4,262144]{1,0:T(4,128)S(1)} %copy-done, f32[4,1]{1,0:T(4,128)S(1)} %get-tuple-element.222, f32[4,262143]{1,0:T(4,128)} %get-tuple-element.223, f32[4,262081]{1,0:T(4,128)} %get-tuple-element.224, f32[4,63]{1,0:T(4,128)S(1)} %get-tuple-element.225, ...), kind=kLoop, calls=%fused_computation.clone.1 | loop fusion | flops 23068672 | bytes 43515912 | tf_op jit(solution)/shard_map/while/body/eval_jaxpr/sub | solution.py:38
  586.3 7.5 all-to-all-start
  593.8 4.6 copy.27
  617.3 23.3 %fusion.27 = f32[4,262144]{1,0:T(4,128)S(1)} fusion(f32[4,262144]{1,0:T(4,128)S(1)} %bitcast.191, f32[4,258048]{1,0:T(4,128)} %get-tuple-element.142, f32[4,4096]{1,0:T(4,128)S(1)} %get-tuple-element.144, f32[4,4096]{1,0:T(4,128)S(1)} %get-tuple-element.143, f32[4,258048]{1,0:T(4,128)} %get-tuple-element.141, f32[4,63]{1,0:T(4,128)S(1)} %get-tuple-element.138, ...), kind=kLoop, calls=%fused_computation.44 | loop fusion | flops 17825792 | bytes 39321600 | tf_op jit(solution)/shard_map/add | solution.py:28
  661.9 26.1 %all-to-all-done = f32[4,32,8192]{2,0,1:T(4,128)} async-done(((f32[4,32,8192]{2,0,1:T(4,128)}), f32[4,32,8192]{2,0,1:T(4,128)}, u32[]{:S(2)}, u32[]{:S(2)}) %all-to-all-start) | async-done | bytes 4194336 | tf_op jit(solution)/shard_map/all_to_all | solution.py:53
  688.0 6.0 all-to-all-start.1
  694.0 5.5 all_to_all.20
  699.5 7.6 convolution_multiply_fusion.1
  707.1 81.0 %all-to-all-done.1 = f32[32,4,8192]{2,1,0:T(4,128)} async-done(((f32[32,4,8192]{2,1,0:T(4,128)}), f32[32,4,8192]{2,1,0:T(4,128)}, u32[]{:S(2)}, u32[]{:S(2)}) %all-to-all-start.1) | async-done | bytes 4194336 | tf_op jit(solution)/shard_map/all_to_all | solution.py:55
  788.2 5.3 reshape.99
  793.5 7.6 convolution_multiply_fusion
  801.1 9.9 convolution_bitcast_fusion.1
  811.0 5.6 copy.15
  816.6 110.8 %all-reduce.6.cloned.1.call-done = (f32[128,128]{1,0:T(8,128)}, f32[128,128]{1,0:T(8,128)}) async-done(((f32[128,128]{1,0:T(8,128)}, f32[128,128]{1,0:T(8,128)}), (f32[128,128]{1,0:T(8,128)}, f32[128,128]{1,0:T(8,128)})) %all-reduce.6.cloned.1.call-update) | async-done | bytes 131088
  929.1 39.5 %all-reduce.2 = (f32[128]{0:T(128)S(1)}, f32[128]{0:T(128)S(1)}) all-reduce(f32[128]{0:T(128)S(1)} %fusion.30, f32[128]{0:T(128)S(1)} %fusion.31), channel_id=1, replica_groups=mesh['ob'=8,'pt'=4] {'ob','pt'}, use_global_device_ids=true, to_apply=%region_5.6 | all-reduce | flops 256 | bytes 2048 | tf_op jit(solution)/shard_map/psum | solution.py:76
  968.6 10.5 %fusion.13 = f32[128,8192]{0,1:T(8,128)} fusion(f32[128,8192]{1,0:T(8,128)} %reshape.99, f32[128,128]{1,0:T(8,128)S(1)} %copy-done.10, f32[128,8192]{0,1:T(8,128)} %convolution_bitcast_fusion.1, f32[128]{0:T(128)S(1)} %add_divide_fusion), kind=kOutput, calls=%fused_computation.22 | convolution fusion | flops 1612709888 | bytes 12648960 | tf_op jit(solution)/shard_map/dot_general | solution.py:71
  979.2 5.6 copy.16
  (281 shorter events, 350.8 us)
Async XLA Ops:
  9.4 16.8 %copy-start.2 = (f32[4,262144]{1,0:T(4,128)}, f32[4,262144]{1,0:T(4,128)S(1)}, u32[]{:S(2)}) copy-start(f32[4,262144]{1,0:T(4,128)S(1)} %copy.77) | copy-start | bytes 12582916
  26.6 6.7 copy-start.6
  26.6 6.7 copy-start.8
  28.6 4.7 copy-start.4
  76.9 4.6 copy-start.3
  113.9 2.7 copy-start
  124.8 4.6 copy-start.3
  161.9 2.7 copy-start
  172.8 4.6 copy-start.3
  209.9 2.7 copy-start
  220.8 4.6 copy-start.3
  257.9 2.7 copy-start
  268.8 4.6 copy-start.3
  316.8 4.6 copy-start.3
  364.8 4.6 copy-start.3
  401.8 2.7 copy-start
  412.8 4.6 copy-start.3
  449.8 2.7 copy-start
  460.7 4.6 copy-start.3
  497.8 2.7 copy-start
  508.7 4.6 copy-start.3
  556.7 4.6 copy-start.3
  586.3 101.6 %all-to-all-start = ((f32[4,32,8192]{2,0,1:T(4,128)}), f32[4,32,8192]{2,0,1:T(4,128)}, u32[]{:S(2)}, u32[]{:S(2)}) async-start(f32[4,32,8192]{2,0,1:T(4,128)} %bitcast.180), calls=%async_computation | async-start | bytes 8388608 | tf_op jit(solution)/shard_map/all_to_all | solution.py:53
  614.6 2.7 copy-start.5
  614.6 2.7 copy-start.7
  614.6 2.7 copy-start.9
  688.0 100.2 %all-to-all-start.1 = ((f32[32,4,8192]{2,1,0:T(4,128)}), f32[32,4,8192]{2,1,0:T(4,128)}, u32[]{:S(2)}, u32[]{:S(2)}) async-start(f32[32,4,8192]{2,1,0:T(4,128)} %fusion.37), calls=%async_computation.1 | async-start | bytes 8388608 | tf_op jit(solution)/shard_map/all_to_all | solution.py:55
  694.0 233.4 %all-reduce.6.cloned.1.call-start = ((), (), s32[]{:S(2)}) async-start(), calls=%async_computation.2 | async-start | bytes 262144
  793.5 7.6 copy-start.10
  928.0 51.1 %copy-start.11 = (f32[4,128]{1,0:T(4,128)}, f32[4,128]{1,0:T(4,128)S(1)}, u32[]{:S(2)}) copy-start(f32[4,128]{1,0:T(4,128)S(1)} %constant_dynamic-slice_fusion) | copy-start | bytes 6148
  928.7 50.4 %copy-start.12 = (f32[4,128]{1,0:T(4,128)}, f32[4,128]{1,0:T(4,128)S(1)}, u32[]{:S(2)}) copy-start(f32[4,128]{1,0:T(4,128)S(1)} %constant_dynamic-slice_fusion.1) | copy-start | bytes 6148
  968.6 10.5 %copy-start.13 = (f32[128]{0:T(128)}, f32[128]{0:T(128)S(1)}, u32[]{:S(2)}) copy-start(f32[128]{0:T(128)S(1)} %add_divide_fusion) | copy-start | bytes 1540
  (5 other events, 13.1 us)
Sparse Core Ops, SparseCore 0:
  801.2 126.1 all-reduce.5
